TPU v7x, 1024 devices: a whole 4x4x32 slice. The times are simulated.
1024 devices in a mesh: enc: 16 (over y, x), seq: 64 (over z, core).
Axes of the slice: x: 4, y: 4, z: 32, core: 2. Of those that a mesh axis runs over, the one named last changes fastest.
Arguments:
- qkv: bfloat16 [64, 4096, 3840], P('enc', 'seq'), may hold values from -6 to 6
- resid: bfloat16 [64, 4096, 1280], P('enc', 'seq'), may hold values from -6 to 6
- block_count: int32 [16, 64], P('enc', 'seq'), may hold values from 2 to 4, as said below
- send_count: int32 [16, 64], P('enc', 'seq'), may hold values from 0 to 1, as said below
- send_slot: int32 [16, 3072], P('enc', 'seq'), may hold values from 0 to 63, as said below
- lm_row: int32 [16, 4096], P('enc', 'seq'), may hold values from -1 to 47, as said below
- out_weight: bfloat16 [1280, 1280], replicated, may hold values from -0.15625 to 0.15625
- out_bias: bfloat16 [1280], replicated, may hold values from -3 to 3
- norm_gain: bfloat16 [1280], replicated, may hold values from 0.25 to 1.75
Outputs:
- lm_tokens: bfloat16 [16, 3072, 5120], P('enc', 'seq')
Inputs may be any that keep to these rules, and one draw needn't show every extreme that they name: send_count is at most 1; a device's live slots come first. block_count[e, g] = 3 + send_count[e, g] - send_count[(e - 1) mod 16, g]. `send_slot`: values of one device are distinct; with o = (s - g) mod 64 and finv(o) = 2 * o for o < 32, else 2 * (o - 32) + 1, the device at seq index g uses slot s + k exactly when k * 64 + finv(o) < 48. `lm_row`: at seq index s, with o and finv as for send_slot, arriving slot g + k holds -1 exactly when k * 64 + finv((s - g) mod 64) >= 48; the other slots hold each of 0 to 47 once.
All inputs are finite; a program needn't handle non-finite values.
Results may differ from a plain program's by a relative error of at most 0.0036.
Values may be sent and summed in bfloat16 or wider, within the bound.
A program may use at most 32 MiB of HBM per device.

v0:
```python
import math

import jax
import jax.numpy as jnp
from jax import lax
from jax.sharding import PartitionSpec as P

HEADS = 16
WIN = 64


def from_behind(block, axis, distance):
    devices = range(lax.axis_size(axis))
    route = [((i - distance) % len(devices), i) for i in devices]
    return lax.ppermute(block, axis, route)


def encode_blocks(qkv_blocks, resid_blocks, out_weight, out_bias, norm_gain):
    block_total = qkv_blocks.shape[0]
    window_len = qkv_blocks.shape[1]
    model_width = resid_blocks.shape[2]
    head_size = model_width // HEADS
    queries = qkv_blocks[:, :, :model_width].reshape(block_total, window_len, HEADS, head_size)
    key_rows = qkv_blocks[:, :, model_width : 2 * model_width].reshape(
        block_total, window_len, HEADS, head_size
    )
    value_rows = qkv_blocks[:, :, 2 * model_width :].reshape(
        block_total, window_len, HEADS, head_size
    )
    scores = jnp.einsum(
        "bqhd,bkhd->bhqk", queries, key_rows, preferred_element_type=jnp.float32
    ) * (1.0 / math.sqrt(head_size))
    exp_scores = jnp.exp(scores - jnp.max(scores, axis=-1, keepdims=True))
    probabilities = (exp_scores / jnp.sum(exp_scores, axis=-1, keepdims=True)).astype(jnp.bfloat16)
    attended = jnp.einsum(
        "bhqk,bkhd->bqhd", probabilities, value_rows, preferred_element_type=jnp.float32
    ).astype(jnp.bfloat16)
    flat_rows = attended.reshape(block_total * window_len, model_width)
    hidden = jnp.dot(flat_rows, out_weight, preferred_element_type=jnp.float32)
    hidden = (
        hidden
        + out_bias.astype(jnp.float32)
        + resid_blocks.reshape(block_total * window_len, model_width).astype(jnp.float32)
    )
    inv_rms = lax.rsqrt(jnp.mean(hidden * hidden, axis=-1, keepdims=True) + 1e-06)
    normed = (hidden * inv_rms * norm_gain.astype(jnp.float32)).astype(jnp.bfloat16)
    return normed.reshape(block_total, window_len // 4, 4 * model_width)


def per_device(
    qkv, resid, block_count, send_count, send_slot, lm_row, out_weight, out_bias, norm_gain
):
    slot_total = qkv.shape[0]
    model_width = resid.shape[2]
    row_total = send_slot.shape[1]
    blocks_used = row_total // (WIN // 4)
    spare_slots = slot_total - blocks_used
    arrive_total = lm_row.shape[1]
    live_blocks = block_count[0, 0]
    kept_blocks = live_blocks - send_count[0, 0]
    work_index = jnp.arange(blocks_used, dtype=jnp.int32)
    source_index = jnp.where(
        work_index < kept_blocks, work_index, work_index + slot_total + spare_slots - blocks_used
    )
    lend_start = live_blocks - spare_slots
    both_parts = jnp.concatenate([qkv, resid], axis=2)
    outgoing_blocks = lax.dynamic_slice_in_dim(both_parts, lend_start, spare_slots, 0)
    borrowed = from_behind(outgoing_blocks, "enc", 1)
    combined = jnp.take(jnp.concatenate([both_parts, borrowed], axis=0), source_index, axis=0)
    merged = encode_blocks(
        combined[:, :, : 3 * model_width],
        combined[:, :, 3 * model_width :],
        out_weight,
        out_bias,
        norm_gain,
    )
    work_rows = merged.reshape(row_total, merged.shape[2])
    slot_ids = jnp.arange(arrive_total, dtype=jnp.int32)
    sending_map = (send_slot[0][:, None] == slot_ids[None, :]).astype(jnp.bfloat16)
    outgoing = jnp.einsum(
        "rc,rd->cd", sending_map, work_rows, preferred_element_type=jnp.float32
    ).astype(jnp.bfloat16)
    arrived = lax.all_to_all(outgoing, "seq", split_axis=0, concat_axis=0, tiled=True)
    row_ids = jnp.arange(row_total, dtype=jnp.int32)
    placing_map = (lm_row[0][:, None] == row_ids[None, :]).astype(jnp.bfloat16)
    placed = jnp.einsum("cr,cd->rd", placing_map, arrived, preferred_element_type=jnp.float32)
    return placed.astype(jnp.bfloat16)[None]


def solution(mesh):
    placed = (
        P("enc", "seq", None),
        P("enc", "seq", None),
        P("enc", "seq"),
        P("enc", "seq"),
        P("enc", "seq"),
        P("enc", "seq"),
        P(),
        P(),
        P(),
    )
    return jax.shard_map(
        per_device, mesh=mesh, in_specs=placed, out_specs=P("enc", "seq", None), check_vma=False
    )
```

profile of v0, /device:TPU:1, one launch (start us, length us, event | category | flops | bytes accessed | tf_op | source)
XLA Modules:
  0.0 189.6 jit_solution(14258769633338095687)
XLA Ops:
  0.0 0.0 copy-start
  0.8 3.2 %constant_dynamic-update-slice_fusion.1 = bf16[4,64,5120]{2,1,0:T(8,128)(2,1)} fusion(bf16[4,64,3840]{2,1,0:T(8,128)(2,1)} %param.9), kind=kLoop, calls=%fused_computation.30 | loop fusion | bytes 3932160
  4.0 2.0 %constant_dynamic-update-slice_fusion = bf16[4,64,5120]{2,1,0:T(8,128)(2,1)} fusion(bf16[4,64,5120]{2,1,0:T(8,128)(2,1)} %constant_dynamic-update-slice_fusion.1, bf16[4,64,1280]{2,1,0:T(8,128)(2,1)} %param.10), kind=kLoop, calls=%fused_computation.29 | loop fusion | bytes 1310720 | tf_op jit(solution)/shard_map/concatenate | solution.py:66
  6.0 1.1 constant_dynamic-slice_fusion
  7.1 3.9 %collective-permute-start = (bf16[1,64,5120]{2,1,0:T(8,128)(2,1)S(1)}, bf16[1,64,5120]{2,1,0:T(8,128)(2,1)S(1)}, u32[]{:S(2)}, u32[]{:S(2)}) collective-permute-start(bf16[1,64,5120]{2,1,0:T(8,128)(2,1)S(1)} %constant_dynamic-slice_fusion), channel_id=1, source_target_pairs={{960,0},{0,64},{64,128},{128,192},{192,256},{256,320},{320,384},{3... | collective-permute-start | bytes 1966088 | tf_op jit(solution)/shard_map/ppermute | solution.py:15
  11.7 0.0 copy-done.1
  11.8 0.0 copy-done.2
  11.8 10.9 %collective-permute-done = bf16[1,64,5120]{2,1,0:T(8,128)(2,1)S(1)} collective-permute-done((bf16[1,64,5120]{2,1,0:T(8,128)(2,1)S(1)}, bf16[1,64,5120]{2,1,0:T(8,128)(2,1)S(1)}, u32[]{:S(2)}, u32[]{:S(2)}) %collective-permute-start) | collective-permute-done | bytes 655392 | tf_op jit(solution)/shard_map/ppermute | solution.py:15
  22.8 3.7 %pad_maximum_fusion = bf16[5,64,5120]{2,1,0:T(8,128)(2,1)} fusion(bf16[1,64,5120]{2,1,0:T(8,128)(2,1)S(1)} %collective-permute-done, bf16[4,64,5120]{2,1,0:T(8,128)(2,1)} %constant_dynamic-update-slice_fusion), kind=kLoop, calls=%fused_computation.6 | loop fusion | flops 1638400 | bytes 6553600 | tf_op jit(solution)/shard_map/concatenate | solution.py:69
  26.5 4.0 %gather_fusion = bf16[3,64,5120]{2,1,0:T(8,128)(2,1)} fusion(bf16[5,64,5120]{2,1,0:T(8,128)(2,1)} %pad_maximum_fusion, s32[1024]{0:T(1024)S(1)} %pad_clamp_fusion), kind=kCustom, calls=%fused_computation | custom fusion | bytes 3932172 | tf_op jit(solution)/shard_map/jit(_take)/gather | solution.py:69
  30.5 1.8 broadcast_select_fusion
  32.3 1.3 fusion.22
  33.6 2.8 %reshape.70 = bf16[3,64,16,80]{3,2,1,0:T(8,128)(2,1)} reshape(bf16[3,64,1280]{2,1,0:T(8,128)(2,1)} %get-tuple-element.7) | data formatting | bytes 983040 | tf_op jit(solution)/shard_map/reshape | solution.py:23
  36.4 2.8 %reshape.71 = bf16[3,64,16,80]{3,2,1,0:T(8,128)(2,1)} reshape(bf16[3,64,1280]{2,1,0:T(8,128)(2,1)} %get-tuple-element.6) | data formatting | bytes 983040 | tf_op jit(solution)/shard_map/reshape | solution.py:24
  39.2 3.1 %convolution_multiply_fusion = f32[3,16,64,64]{2,3,1,0:T(8,128)} fusion(bf16[3,64,16,80]{3,2,1,0:T(8,128)(2,1)} %reshape.71, bf16[3,64,16,80]{3,2,1,0:T(8,128)(2,1)} %reshape.70), kind=kOutput, calls=%fused_computation.12 | convolution fusion | flops 31653888 | bytes 1769472 | tf_op jit(solution)/shard_map/bqhd,bkhd->bhqk/dot_general | solution.py:30
  42.3 2.2 %fusion.23 = f32[3,16,64]{2,1,0:T(8,128)S(1)} fusion(bf16[3,64,16,80]{3,2,1,0:T(8,128)(2,1)} %reshape.71, bf16[3,64,16,80]{3,2,1,0:T(8,128)(2,1)} %reshape.70), kind=kOutput, calls=%fused_computation.42 | convolution fusion | flops 32047168 | bytes 995328 | tf_op jit(solution)/shard_map/sub | solution.py:33
  44.5 2.8 %reshape.69 = bf16[3,64,16,80]{3,2,1,0:T(8,128)(2,1)} reshape(bf16[3,64,1280]{2,1,0:T(8,128)(2,1)} %get-tuple-element.8) | data formatting | bytes 983040 | tf_op jit(solution)/shard_map/reshape | solution.py:27
  47.3 3.7 %fusion.6 = bf16[3,64,16,80]{3,1,2,0:T(8,128)(2,1)} fusion(bf16[3,64,16,80]{3,2,1,0:T(8,128)(2,1)} %reshape.69, f32[3,16,64]{2,1,0:T(8,128)S(1)} %fusion.23, f32[3,16,64,64]{2,3,1,0:T(8,128)} %convolution_multiply_fusion), kind=kOutput, calls=%fused_computation.15 | convolution fusion | flops 32296000 | bytes 1781760 | tf_op jit(solution)/shard_map/bhqk,bkhd->bqhd/dot_general | solution.py:35
  50.9 2.5 %copy.26 = bf16[3,64,16,80]{3,2,1,0:T(8,128)(2,1)} copy(bf16[3,64,16,80]{3,1,2,0:T(8,128)(2,1)} %fusion.6) | data formatting | bytes 983040 | tf_op jit(solution)/shard_map/convert_element_type | solution.py:37
  53.5 2.6 %reshape.72 = bf16[192,1280]{1,0:T(8,128)(2,1)} reshape(bf16[3,64,16,80]{3,2,1,0:T(8,128)(2,1)} %copy.26) | data formatting | bytes 983040 | tf_op jit(solution)/shard_map/reshape | solution.py:38
  56.0 0.0 copy-done
  56.0 2.1 %multiply_reduce_fusion = (f32[192]{0:T(256)S(1)}, f32[192,1280]{1,0:T(8,128)S(1)}) fusion(bf16[192,1280]{1,0:T(8,128)(2,1)} %bitcast.24, f32[1280]{0:T(1024)S(1)} %convert_element_type.35, bf16[192,1280]{1,0:T(8,128)(2,1)} %reshape.72, bf16[1280,1280]{1,0:T(8,128)(2,1)S(1)} %copy-done), kind=kOutput, calls=%fused_computation.17 | convolution fusion | flops 630374208 | bytes 5248768 | tf_op jit(solution)/shard_map/dot_general | solution.py:39
  58.1 0.0 copy-start.3
  58.2 0.9 multiply_convert_fusion
  59.1 2.1 %reshape_reshape.3 = bf16[48,5120]{1,0:T(8,128)(2,1)} reshape(bf16[192,1280]{1,0:T(8,128)(2,1)} %multiply_convert_fusion) | data formatting | bytes 983040 | tf_op jit(solution)/shard_map/reshape;reshape | solution.py:77
  61.2 2.3 %fusion.1 = bf16[64,1,5120]{2,0,1:T(8,128)(2,1)} fusion(bf16[48,5120]{1,0:T(8,128)(2,1)} %reshape_reshape.3, s32[48]{0:T(128)S(1)} %bitcast.25), kind=kOutput, calls=%fused_computation.4 | convolution fusion | flops 31788032 | bytes 1147072 | tf_op jit(solution)/shard_map/rc,rd->cd/dot_general | solution.py:80
  63.5 0.5 broadcast.79
  64.0 2.9 %reduce = bf16[64,5120]{1,0:T(8,128)(2,1)} reduce(bf16[64,1,5120]{2,0,1:T(8,128)(2,1)} %fusion.1, bf16[]{:T(256)} %broadcast.79), dimensions={1}, to_apply=%copy.27.reduce_sub_computation | reduce | bytes 1310722 | tf_op jit(solution)/shard_map/all_to_all | solution.py:83
  66.9 3.0 %reshape.82 = bf16[64,2,2560]{2,1,0:T(2,128)(2,1)} reshape(bf16[64,5120]{1,0:T(8,128)(2,1)} %reduce) | data formatting | bytes 1310720
  69.9 112.2 %all_to_all.12 = bf16[64,2,2560]{2,1,0:T(2,128)(2,1)} all-to-all(bf16[64,2,2560]{2,1,0:T(2,128)(2,1)} %reshape.82), channel_id=1, replica_groups=mesh['enc'=16,'seq'=64] {'seq'}, dimensions={0} | all-to-all | bytes 1310720 | tf_op jit(solution)/shard_map/all_to_all | solution.py:83
  182.1 5.0 %reshape.83 = bf16[64,1,5120]{2,1,0:T(2,128)(2,1)} reshape(bf16[64,2,2560]{2,1,0:T(2,128)(2,1)} %all_to_all.12) | data formatting | bytes 1310720
  187.1 2.5 %fusion.2 = bf16[1,48,5120]{2,1,0:T(8,128)(2,1)} fusion(bf16[64,1,5120]{2,1,0:T(2,128)(2,1)} %reshape.83, s32[64]{0:T(128)S(1)} %bitcast.26), kind=kOutput, calls=%fused_computation.5 | convolution fusion | flops 31706112 | bytes 1147136 | tf_op jit(solution)/shard_map/cr,cd->rd/dot_general | solution.py:86
  (11 shorter events, 0.0 us)
Async XLA Ops:
  0.0 56.0 %copy-start = (bf16[1280,1280]{1,0:T(8,128)(2,1)S(1)}, bf16[1280,1280]{1,0:T(8,128)(2,1)}, u32[]{:S(2)}) copy-start(bf16[1280,1280]{1,0:T(8,128)(2,1)} %param.15) | copy-start | bytes 9830404
  4.0 7.8 %copy-start.1 = (bf16[1280]{0:T(1024)(128)(2,1)S(1)}, bf16[1280]{0:T(1024)(128)(2,1)}, u32[]{:S(2)}) copy-start(bf16[1280]{0:T(1024)(128)(2,1)} %param.16) | copy-start | bytes 7684
  4.0 7.8 %copy-start.2 = (bf16[1280]{0:T(1024)(128)(2,1)S(1)}, bf16[1280]{0:T(1024)(128)(2,1)}, u32[]{:S(2)}) copy-start(bf16[1280]{0:T(1024)(128)(2,1)} %param.17) | copy-start | bytes 7684
  7.1 15.6 %collective-permute-start = (bf16[1,64,5120]{2,1,0:T(8,128)(2,1)S(1)}, bf16[1,64,5120]{2,1,0:T(8,128)(2,1)S(1)}, u32[]{:S(2)}, u32[]{:S(2)}) collective-permute-start(bf16[1,64,5120]{2,1,0:T(8,128)(2,1)S(1)} %constant_dynamic-slice_fusion), channel_id=1, source_target_pairs={{960,0},{0,64},{64,128},{128,192},{192,256},{256,320},{320,384},{3... | collective-permute-start | bytes 1966088 | tf_op jit(solution)/shard_map/ppermute | solution.py:15
  58.1 3.1 %copy-start.3 = (s32[1,48]{1,0:T(1,128)S(1)}, s32[1,48]{1,0:T(1,128)}, u32[]{:S(2)}) copy-start(s32[1,48]{1,0:T(1,128)} %param.13) | copy-start | bytes 580
  69.9 117.2 %copy-start.4 = (s32[1,64]{1,0:T(1,128)S(1)}, s32[1,64]{1,0:T(1,128)}, u32[]{:S(2)}) copy-start(s32[1,64]{1,0:T(1,128)} %param.14) | copy-start | bytes 772
where the time goes:
time: 191 us; the launch traced here: 190 us
  blocking collectives  112 us (59%)
  local copies, waits for them, and re-layouts  35.7 us (19%)
  matrix products  15.8 us (8%)
  waiting for transfers between devices  10.9 us (6%)
  other arithmetic  9.35 us (5%)
  starting transfers between devices  3.95 us (2%)
    all_to_all x1, blocking collectives, per_device(): lax.all_to_all(outgoing, 'seq', split_axis=0, concat_axis=0, tiled=True)  112 us
    unnamed x13, local copies, waits for them, and re-layouts  11.1 us
    ppermute x1, waiting for transfers between devices, from_behind(): return lax.ppermute(block, axis, route)  10.9 us
    gather x1, local copies, waits for them, and re-layouts, per_device(): jnp.take(jnp.concatenate([both_parts, borrowed], axis=0), source_index, a...  3.99 us
    ppermute x1, starting transfers between devices, from_behind(): return lax.ppermute(block, axis, route)  3.95 us
  transfers between devices with their start and end apart: 1, of which 1 were waited for; matrix products, arithmetic and copies ran while one was open for 0% of the time, Pallas kernels for 0%

commit v1 on v0

v1 whole, which is shorter than its diff:
```python
import functools
import math

import jax
import jax.numpy as jnp
from jax import lax
from jax.experimental import pallas as pl
from jax.experimental.pallas import tpu as pltpu
from jax.sharding import PartitionSpec as P

MESH = pl.DeviceIdType.MESH
D = 1280
HALF = 640
HEAD = 80
WIN = 64
SEQ = 64
ENC = 16
TOK = 48
JUMP = 8
MOVED = (32, 33, 34)

UP = list(range(1, 24)) + list(MOVED)
DOWN = [o - 64 for o in range(55, 31, -1) if o not in MOVED]
OFFSETS = [0] + UP + DOWN


def full_jumps(offset):
    return (abs(offset) - 1) // JUMP if offset else 0


def jump_groups():
    groups = []
    i = 1
    while i < TOK:
        sign = 1 if OFFSETS[i] > 0 else -1
        jumps = full_jumps(OFFSETS[i])
        k = i
        while k < TOK and OFFSETS[k] * sign > 0 and full_jumps(OFFSETS[k]) == jumps:
            k += 1
        if jumps:
            groups.append((sign, jumps, i, k))
        i = k
    return groups


GROUPS = jump_groups()
ROUNDS = max(g[1] for g in GROUPS)


def last_offset(offset):
    sign = 1 if offset > 0 else -1
    return offset - sign * JUMP * full_jumps(offset)


PARTNERS = sorted(
    {last_offset(o) for o in OFFSETS if o} | {sign * JUMP for sign, _, _, _ in GROUPS}
)


def send_order():
    up = [i for i, g in enumerate(GROUPS) if g[0] > 0]
    down = [i for i, g in enumerate(GROUPS) if g[0] < 0]

    def far_first(ids):
        return sorted(ids, key=lambda i: (-GROUPS[i][1], -i))

    def weave(a, b):
        out = []
        for i in range(max(len(a), len(b))):
            out += b[i : i + 1] + a[i : i + 1]
        return out

    order = weave([("jump", i, 1) for i in far_first(up)], [("jump", i, 1) for i in far_first(down)])
    for turn in range(2, ROUNDS + 2):
        lanes = []
        for ids in (up, down):
            lane = []
            for i in far_first(ids):
                _, jumps, first, end = GROUPS[i]
                if jumps >= turn:
                    lane.append(("jump", i, turn))
                elif jumps == turn - 1:
                    lane += [("last", t) for t in range(end - 1, first - 1, -1)]
            lanes.append(lane)
        order += weave(*lanes)
        if turn == 2:
            order += [("last", t) for t in range(1, TOK) if full_jumps(OFFSETS[t]) == 0]
    return order


ORDER = send_order()


def place_offset(place):
    n_up = len(UP)
    return jnp.where(place < 24, place, jnp.where(place <= n_up, place + 8, 82 - place))


def encode_kernel(
    qkv_hbm,
    resid_hbm,
    count_ref,
    lent_ref,
    slot_ref,
    weight_hbm,
    bias_ref,
    gain_ref,
    out_hbm,
    qkv,
    resid,
    weight,
    att,
    lend,
    normed,
    outgoing,
    relay,
    load_sem,
    lend_sem,
    jump_send,
    jump_recv,
    last_send,
    last_recv,
    own_sem,
):
    me = lax.axis_index("seq")
    enc = lax.axis_index("enc")

    def along_seq(offset):
        return (enc, lax.rem(me + (offset % SEQ), SEQ))

    next_enc = (lax.rem(enc + 1, ENC), me)
    prev_enc = (lax.rem(enc + ENC - 1, ENC), me)

    barrier = pltpu.get_barrier_semaphore()
    for offset in PARTNERS:
        pl.semaphore_signal(barrier, inc=1, device_id=along_seq(-offset), device_id_type=MESH)
    pl.semaphore_signal(barrier, inc=1, device_id=prev_enc, device_id_type=MESH)

    loads = [
        pltpu.make_async_copy(qkv_hbm, qkv, load_sem.at[0]),
        pltpu.make_async_copy(weight_hbm, weight, load_sem.at[1]),
        pltpu.make_async_copy(resid_hbm, resid, load_sem.at[2]),
    ]
    for copy in loads:
        copy.start()

    live = count_ref[0, 0]
    kept = live - lent_ref[0, 0]
    last_live = jnp.clip(live - 1, 0, 3)
    bias = bias_ref[...].astype(jnp.float32)
    gain = gain_ref[...].astype(jnp.float32)

    col = lax.broadcasted_iota(jnp.int32, (1, 4 * WIN), 1)
    row48 = lax.broadcasted_iota(jnp.int32, (TOK, 4 * WIN), 0)
    col48 = lax.broadcasted_iota(jnp.int32, (TOK, 4 * WIN), 1)
    work_row = jnp.where(col48 < 3 * WIN, col48 // 4, (col48 - WIN) // 4)
    spread = (row48 == work_row).astype(jnp.bfloat16)
    slots = jnp.broadcast_to(slot_ref[...].astype(jnp.float32), (8, TOK)).astype(jnp.bfloat16)
    col_slot = jnp.dot(slots, spread, preferred_element_type=jnp.float32)[0:1].astype(jnp.int32)
    usable = jnp.where(col < 2 * WIN, 2, jnp.where(col < 3 * WIN, kept, 5 - kept)) >= jnp.where(
        col < 2 * WIN, 0, 3
    )
    col_slot = jnp.where(usable, col_slot, -1)

    half_scale = math.log2(math.e) / math.sqrt(HEAD)
    lane = lax.broadcasted_iota(jnp.int32, (1, 256), 1)
    head_mask = []
    ones_mask = []
    row128 = lax.broadcasted_iota(jnp.int32, (128, 256), 0)
    lane128 = lax.broadcasted_iota(jnp.int32, (128, 256), 1)
    for pair in range(4):
        low = 32 * pair
        first = ((lane >= low) & (lane < low + HEAD)).astype(jnp.bfloat16)
        second = ((lane >= low + HEAD) & (lane < low + 2 * HEAD)).astype(jnp.bfloat16)
        head_mask.append((first, second))
        start = jnp.where(row128 < WIN, low, low + HEAD)
        ones_mask.append(((lane128 >= start) & (lane128 < start + HEAD)).astype(jnp.bfloat16))
    left = lax.broadcasted_iota(jnp.int32, (WIN, 128), 1) < WIN

    def attend(slot, row):
        for group in range(2):
            num = [None] * 5
            den = [None] * 5
            for pair in range(4):
                at = HALF * group + 128 * pair
                q = qkv[slot, :, at : at + 256]
                k = qkv[slot, :, D + at : D + at + 256]
                v = qkv[slot, :, 2 * D + at : 2 * D + at + 256]
                first, second = head_mask[pair]
                keys = jnp.concatenate([k * first, k * second], axis=0)
                s = lax.dot_general(
                    q, keys, (((1,), (1,)), ((), ())), preferred_element_type=jnp.float32
                )
                top_a = jnp.max(jnp.where(left, s, -jnp.inf), axis=1, keepdims=True)
                top_b = jnp.max(jnp.where(left, -jnp.inf, s), axis=1, keepdims=True)
                p = jnp.exp2((s - jnp.where(left, top_a, top_b)) * half_scale).astype(jnp.bfloat16)
                values = jnp.concatenate([v * first, v * second], axis=0)
                o = jnp.dot(p, values, preferred_element_type=jnp.float32)
                total = jnp.dot(p, ones_mask[pair], preferred_element_type=jnp.float32)
                for part in range(2):
                    cut = slice(128 * part, 128 * part + 128)
                    tile = pair + part
                    num[tile] = o[:, cut] if num[tile] is None else num[tile] + o[:, cut]
                    den[tile] = total[:, cut] if den[tile] is None else den[tile] + total[:, cut]
            for tile in range(5):
                at = HALF * group + 128 * tile
                att[pl.ds(row, WIN), at : at + 128] = (num[tile] / den[tile]).astype(jnp.bfloat16)

    def project(rows, resid_rows):
        hidden = jnp.dot(att[0:rows], weight[...], preferred_element_type=jnp.float32)
        hidden = hidden + bias + resid_rows.astype(jnp.float32)
        inv_rms = lax.rsqrt(jnp.mean(hidden * hidden, axis=-1, keepdims=True) + 1e-06)
        return (hidden * inv_rms * gain).astype(jnp.bfloat16)

    loads[0].wait()
    attend(last_live, 0)
    loads[1].wait()
    loads[2].wait()
    lend[...] = project(WIN, resid[last_live])

    pl.semaphore_wait(barrier, len(PARTNERS) + 1)
    lending = pltpu.make_async_remote_copy(
        src_ref=lend,
        dst_ref=normed.at[pl.ds(3 * WIN, WIN)],
        send_sem=lend_sem.at[0],
        recv_sem=lend_sem.at[1],
        device_id=next_enc,
        device_id_type=MESH,
    )
    lending.start()

    for block in range(3):
        attend(block, WIN * block)
    normed[0 : 3 * WIN] = project(3 * WIN, resid[0:3].reshape(3 * WIN, D))

    r = lax.broadcasted_iota(jnp.int32, (TOK * 8, 4 * WIN), 0)
    c = lax.broadcasted_iota(jnp.int32, (TOK * 8, 4 * WIN), 1)
    target = (me + place_offset(r // 8)) & (SEQ - 1)
    hit = (target == col_slot) & ((r & 3) == (c & 3))
    pick_low = (hit & ((r & 4) == 0)).astype(jnp.bfloat16)
    pick_high = (hit & ((r & 4) != 0)).astype(jnp.bfloat16)

    lending.wait()
    placed = jnp.dot(pick_low, normed[:, :HALF], preferred_element_type=jnp.float32)
    placed = placed + jnp.dot(pick_high, normed[:, HALF:], preferred_element_type=jnp.float32)
    outgoing[...] = placed.astype(jnp.bfloat16).reshape(TOK, 8, HALF)

    own = pltpu.make_async_copy(outgoing.at[0], out_hbm.at[0], own_sem)
    own.start()

    jumps = {}
    arrived = set()
    lasts = []
    group_of = {t: i for i, g in enumerate(GROUPS) for t in range(g[2], g[3])}

    def held(first, count, done):
        if done == 0:
            return outgoing.at[pl.ds(first, count)]
        return relay.at[done - 1, pl.ds(first, count)]

    def need(group, done):
        if done and (group, done) not in arrived:
            arrived.add((group, done))
            jumps[group, done].wait_recv()

    for item in ORDER:
        if item[0] == "jump":
            _, group, turn = item
            sign, _, first, end = GROUPS[group]
            need(group, turn - 1)
            sem = group * ROUNDS + turn - 1
            copy = pltpu.make_async_remote_copy(
                src_ref=held(first, end - first, turn - 1),
                dst_ref=relay.at[turn - 1, pl.ds(first, end - first)],
                send_sem=jump_send.at[sem],
                recv_sem=jump_recv.at[sem],
                device_id=along_seq(sign * JUMP),
                device_id_type=MESH,
            )
            copy.start()
            jumps[group, turn] = copy
        else:
            token = item[1]
            done = full_jumps(OFFSETS[token])
            if done:
                need(group_of[token], done)
            copy = pltpu.make_async_remote_copy(
                src_ref=held(token, 1, done),
                dst_ref=out_hbm.at[pl.ds(token, 1)],
                send_sem=last_send.at[token],
                recv_sem=last_recv.at[token],
                device_id=along_seq(last_offset(OFFSETS[token])),
                device_id_type=MESH,
            )
            copy.start()
            lasts.append(copy)
    own.wait()
    for copy in jumps.values():
        copy.wait_send()
    for copy in lasts:
        copy.wait()


def place_kernel(row_ref, arrived_ref, out_ref):
    me = lax.axis_index("seq")
    rows = TOK * 8
    g = lax.broadcasted_iota(jnp.int32, (SEQ, rows), 0)
    c = lax.broadcasted_iota(jnp.int32, (SEQ, rows), 1)
    sender = (me - place_offset(c // 8)) & (SEQ - 1)
    lm = jnp.broadcast_to(row_ref[...].astype(jnp.float32), (8, SEQ)).astype(jnp.bfloat16)
    row_of = jnp.dot(lm, (g == sender).astype(jnp.bfloat16), preferred_element_type=jnp.float32)
    row_of = row_of[0:1].astype(jnp.int32)
    r = lax.broadcasted_iota(jnp.int32, (TOK, rows), 0)
    c = lax.broadcasted_iota(jnp.int32, (TOK, rows), 1)
    hit = r == row_of
    arrived = arrived_ref[...].reshape(rows, HALF)
    for part in range(8):
        half, patch = part // 4, part % 4
        pick = (hit & ((c & 7) == part)).astype(jnp.bfloat16)
        cut = jnp.dot(pick, arrived, preferred_element_type=jnp.float32)
        at = patch * D + half * HALF
        out_ref[:, at : at + HALF] = cut.astype(jnp.bfloat16)


def per_device(
    qkv, resid, block_count, send_count, send_slot, lm_row, out_weight, out_bias, norm_gain
):
    vmem = pl.BlockSpec(memory_space=pltpu.VMEM)
    smem = pl.BlockSpec(memory_space=pltpu.SMEM)
    hbm = pl.BlockSpec(memory_space=pl.ANY)
    dma = pltpu.SemaphoreType.DMA
    arrived = pl.pallas_call(
        encode_kernel,
        out_shape=jax.ShapeDtypeStruct((TOK, 8, HALF), jnp.bfloat16),
        in_specs=[hbm, hbm, smem, smem, vmem, hbm, vmem, vmem],
        out_specs=hbm,
        scratch_shapes=[
            pltpu.VMEM(qkv.shape, jnp.bfloat16),
            pltpu.VMEM(resid.shape, jnp.bfloat16),
            pltpu.VMEM((D, D), jnp.bfloat16),
            pltpu.VMEM((3 * WIN, D), jnp.bfloat16),
            pltpu.VMEM((WIN, D), jnp.bfloat16),
            pltpu.VMEM((4 * WIN, D), jnp.bfloat16),
            pltpu.VMEM((TOK, 8, HALF), jnp.bfloat16),
            pltpu.VMEM((ROUNDS, TOK, 8, HALF), jnp.bfloat16),
            dma((3,)),
            dma((2,)),
            dma((len(GROUPS) * ROUNDS,)),
            dma((len(GROUPS) * ROUNDS,)),
            dma((TOK,)),
            dma((TOK,)),
            dma,
        ],
        compiler_params=pltpu.CompilerParams(collective_id=0, has_side_effects=True),
    )(
        qkv,
        resid,
        block_count,
        send_count,
        send_slot,
        out_weight,
        out_bias.reshape(1, D),
        norm_gain.reshape(1, D),
    )
    placed = pl.pallas_call(
        place_kernel,
        out_shape=jax.ShapeDtypeStruct((TOK, 4 * D), jnp.bfloat16),
        in_specs=[vmem, vmem],
        out_specs=vmem,
    )(lm_row, arrived)
    return placed[None]


def solution(mesh):
    placed = (
        P("enc", "seq", None),
        P("enc", "seq", None),
        P("enc", "seq"),
        P("enc", "seq"),
        P("enc", "seq"),
        P("enc", "seq"),
        P(),
        P(),
        P(),
    )
    return jax.shard_map(
        per_device, mesh=mesh, in_specs=placed, out_specs=P("enc", "seq", None), check_vma=False
    )
```

time: 191 us -> 88.9 us (0.47)
  blocking collectives: 112 us -> 0 us
  Pallas kernels: 0 us -> 84.7 us
  local copies, waits for them, and re-layouts: 35.7 us -> 2.57 us
  matrix products: 15.8 us -> 0 us
  waiting for transfers between devices: 10.9 us -> 0 us
  other arithmetic: 9.35 us -> 0 us
  starting transfers between devices: 3.95 us -> 0 us
    all_to_all x1 -> x0, blocking collectives: 112 us -> none  [per_device(): lax.all_to_all(outgoing, 'seq', split_axis=0, concat_axis=0, tiled=True)]
    pallas_call x0 -> x2, Pallas kernels: none -> 84.7 us  [the longest x1 82 us: per_device(): pl.pallas_call(encode_kernel, out_shape=jax.ShapeDtypeStruct((TOK, 8, HAL...]
    dot_general x5 -> x0, matrix products: 13.7 us -> none  [the longest x1 3.66 us: encode_blocks(): jnp.einsum('bhqk,bkhd->bqhd', probabilities, value_rows, preferred_elemen...]
    unnamed x13 -> x0, local copies, waits for them, and re-layouts: 11.1 us -> none
    ppermute x1 -> x0, waiting for transfers between devices: 10.9 us -> none  [from_behind(): return lax.ppermute(block, axis, route)]
    reshape x4 -> x2, local copies, waits for them, and re-layouts: 11 us -> 2.57 us  [the longest x1 1.28 us: per_device(): out_bias.reshape(1, D)]
    gather x1 -> x0, local copies, waits for them, and re-layouts: 3.99 us -> none  [per_device(): jnp.take(jnp.concatenate([both_parts, borrowed], axis=0), source_index, a...]
    ppermute x1 -> x0, starting transfers between devices: 3.95 us -> none  [from_behind(): return lax.ppermute(block, axis, route)]
  transfers between devices with their start and end apart: 1 -> 0, of which waited for: 1 -> 0; matrix products, arithmetic and copies ran while one was open for 0% -> 0% of each run, Pallas kernels for 0% -> 0%
where the time goes in v1:
time: 88.9 us; the launch traced here: 88.6 us
  Pallas kernels  84.7 us (95%)
  local copies, waits for them, and re-layouts  2.57 us (3%)
  between operations  1.31 us (1%)
    pallas_call x1, Pallas kernels, per_device(): pl.pallas_call(encode_kernel, out_shape=jax.ShapeDtypeStruct((TOK, 8, HAL...  82 us
    pallas_call x1, Pallas kernels, per_device(): pl.pallas_call(place_kernel, out_shape=jax.ShapeDtypeStruct((TOK, 4 * D),...  2.72 us

profile of v1, /device:TPU:1, one launch (start us, length us, event | category | flops | bytes accessed | tf_op | source)
XLA Modules:
  0.0 88.6 jit_solution(12060678770702228864)
XLA Ops:
  1.3 1.3 %reshape.6.bias_ref = bf16[1,1280]{1,0:T(2,128)(2,1)} reshape(bf16[1280]{0:T(1024)(128)(2,1)} %param.16) | data formatting | bytes 5120 | tf_op jit(solution)/shard_map/reshape | solution.py:362
  2.6 1.3 %reshape.7.gain_ref = bf16[1,1280]{1,0:T(2,128)(2,1)} reshape(bf16[1280]{0:T(1024)(128)(2,1)} %param.17) | data formatting | bytes 5120 | tf_op jit(solution)/shard_map/reshape | solution.py:363
  3.9 82.0 %shard_map.91.arrived_ref = bf16[48,8,640]{2,1,0:T(8,128)(2,1)} custom-call(bf16[4,64,3840]{2,1,0:T(8,128)(2,1)} %qkv_hbm.1, bf16[4,64,1280]{2,1,0:T(8,128)(2,1)} %resid_hbm.1, s32[1,1]{1,0:T(1,128)S(6)} %copy.10.count_ref, s32[1,1]{1,0:T(1,128)S(6)} %copy.11.lent_ref, s32[1,48]{1,0:T(1,128)} %slot_ref.1, bf16[1280,1280]{1,0:T(8,128)(2,1)} %weight_hbm.1, ...), custom_call_target="tpu_custom_call" | custom-call | tf_op jit(solution)/shard_map/pallas_call | solution.py:332
  85.9 2.7 %shard_map.92 = bf16[48,5120]{1,0:T(8,128)(2,1)} custom-call(s32[1,64]{1,0:T(1,128)} %row_ref.1, bf16[48,8,640]{2,1,0:T(8,128)(2,1)} %shard_map.91.arrived_ref), custom_call_target="tpu_custom_call" | custom-call | tf_op jit(solution)/shard_map/pallas_call | solution.py:365

commit v2 on v1

--- a/solution.py
+++ b/solution.py
@@ -16,84 +16,12 @@
 SEQ = 64
 ENC = 16
 TOK = 48
-JUMP = 8
-MOVED = (32, 33, 34)
-
-UP = list(range(1, 24)) + list(MOVED)
-DOWN = [o - 64 for o in range(55, 31, -1) if o not in MOVED]
-OFFSETS = [0] + UP + DOWN
-
-
-def full_jumps(offset):
-    return (abs(offset) - 1) // JUMP if offset else 0
-
-
-def jump_groups():
-    groups = []
-    i = 1
-    while i < TOK:
-        sign = 1 if OFFSETS[i] > 0 else -1
-        jumps = full_jumps(OFFSETS[i])
-        k = i
-        while k < TOK and OFFSETS[k] * sign > 0 and full_jumps(OFFSETS[k]) == jumps:
-            k += 1
-        if jumps:
-            groups.append((sign, jumps, i, k))
-        i = k
-    return groups
-
-
-GROUPS = jump_groups()
-ROUNDS = max(g[1] for g in GROUPS)
-
-
-def last_offset(offset):
-    sign = 1 if offset > 0 else -1
-    return offset - sign * JUMP * full_jumps(offset)
-
-
-PARTNERS = sorted(
-    {last_offset(o) for o in OFFSETS if o} | {sign * JUMP for sign, _, _, _ in GROUPS}
-)
-
-
-def send_order():
-    up = [i for i, g in enumerate(GROUPS) if g[0] > 0]
-    down = [i for i, g in enumerate(GROUPS) if g[0] < 0]
-
-    def far_first(ids):
-        return sorted(ids, key=lambda i: (-GROUPS[i][1], -i))
-
-    def weave(a, b):
-        out = []
-        for i in range(max(len(a), len(b))):
-            out += b[i : i + 1] + a[i : i + 1]
-        return out
-
-    order = weave([("jump", i, 1) for i in far_first(up)], [("jump", i, 1) for i in far_first(down)])
-    for turn in range(2, ROUNDS + 2):
-        lanes = []
-        for ids in (up, down):
-            lane = []
-            for i in far_first(ids):
-                _, jumps, first, end = GROUPS[i]
-                if jumps >= turn:
-                    lane.append(("jump", i, turn))
-                elif jumps == turn - 1:
-                    lane += [("last", t) for t in range(end - 1, first - 1, -1)]
-            lanes.append(lane)
-        order += weave(*lanes)
-        if turn == 2:
-            order += [("last", t) for t in range(1, TOK) if full_jumps(OFFSETS[t]) == 0]
-    return order
-
-
-ORDER = send_order()
+RELAY = 16
+NEAR = [d for d in range(-RELAY, RELAY + 1) if d]
 
 
 def place_offset(place):
-    n_up = len(UP)
-    return jnp.where(place < 24, place, jnp.where(place <= n_up, place + 8, 82 - place))
+    return jnp.where(place < 24, place, jnp.where(place < 27, place + 8, 82 - place))
 
 
 def encode_kernel(
@@ -116,24 +44,25 @@
     relay,
     load_sem,
     lend_sem,
-    jump_send,
-    jump_recv,
-    last_send,
-    last_recv,
+    relay_send,
+    relay_recv,
+    token_send,
+    token_recv,
     own_sem,
+    far_sem,
 ):
     me = lax.axis_index("seq")
     enc = lax.axis_index("enc")
 
     def along_seq(offset):
-        return (enc, lax.rem(me + (offset % SEQ), SEQ))
+        return (enc, lax.rem(me + offset + 2 * SEQ, SEQ))
 
     next_enc = (lax.rem(enc + 1, ENC), me)
     prev_enc = (lax.rem(enc + ENC - 1, ENC), me)
 
     barrier = pltpu.get_barrier_semaphore()
-    for offset in PARTNERS:
-        pl.semaphore_signal(barrier, inc=1, device_id=along_seq(-offset), device_id_type=MESH)
+    for offset in NEAR:
+        pl.semaphore_signal(barrier, inc=1, device_id=along_seq(offset), device_id_type=MESH)
     pl.semaphore_signal(barrier, inc=1, device_id=prev_enc, device_id_type=MESH)
 
     loads = [
@@ -147,8 +76,8 @@
     live = count_ref[0, 0]
     kept = live - lent_ref[0, 0]
     last_live = jnp.clip(live - 1, 0, 3)
-    bias = bias_ref[...].astype(jnp.float32)
-    gain = gain_ref[...].astype(jnp.float32)
+    bias = bias_ref[...].astype(jnp.float32).reshape(1, D)
+    gain = gain_ref[...].astype(jnp.float32).reshape(1, D)
 
     col = lax.broadcasted_iota(jnp.int32, (1, 4 * WIN), 1)
     row48 = lax.broadcasted_iota(jnp.int32, (TOK, 4 * WIN), 0)
@@ -218,7 +147,8 @@
     loads[2].wait()
     lend[...] = project(WIN, resid[last_live])
 
-    pl.semaphore_wait(barrier, len(PARTNERS) + 1)
+    attend(0, 0)
+    pl.semaphore_wait(barrier, len(NEAR) + 1)
     lending = pltpu.make_async_remote_copy(
         src_ref=lend,
         dst_ref=normed.at[pl.ds(3 * WIN, WIN)],
@@ -228,9 +158,11 @@
         device_id_type=MESH,
     )
     lending.start()
-
-    for block in range(3):
-        attend(block, WIN * block)
+    for offset in (RELAY, -RELAY):
+        pl.semaphore_signal(far_sem, inc=1, device_id=along_seq(offset), device_id_type=MESH)
+
+    attend(1, WIN)
+    attend(2, 2 * WIN)
     normed[0 : 3 * WIN] = project(3 * WIN, resid[0:3].reshape(3 * WIN, D))
 
     r = lax.broadcasted_iota(jnp.int32, (TOK * 8, 4 * WIN), 0)
@@ -248,57 +180,66 @@
     own = pltpu.make_async_copy(outgoing.at[0], out_hbm.at[0], own_sem)
     own.start()
 
-    jumps = {}
-    arrived = set()
-    lasts = []
-    group_of = {t: i for i, g in enumerate(GROUPS) for t in range(g[2], g[3])}
-
-    def held(first, count, done):
-        if done == 0:
-            return outgoing.at[pl.ds(first, count)]
-        return relay.at[done - 1, pl.ds(first, count)]
-
-    def need(group, done):
-        if done and (group, done) not in arrived:
-            arrived.add((group, done))
-            jumps[group, done].wait_recv()
-
-    for item in ORDER:
-        if item[0] == "jump":
-            _, group, turn = item
-            sign, _, first, end = GROUPS[group]
-            need(group, turn - 1)
-            sem = group * ROUNDS + turn - 1
-            copy = pltpu.make_async_remote_copy(
-                src_ref=held(first, end - first, turn - 1),
-                dst_ref=relay.at[turn - 1, pl.ds(first, end - first)],
-                send_sem=jump_send.at[sem],
-                recv_sem=jump_recv.at[sem],
-                device_id=along_seq(sign * JUMP),
-                device_id_type=MESH,
-            )
-            copy.start()
-            jumps[group, turn] = copy
-        else:
-            token = item[1]
-            done = full_jumps(OFFSETS[token])
-            if done:
-                need(group_of[token], done)
-            copy = pltpu.make_async_remote_copy(
-                src_ref=held(token, 1, done),
-                dst_ref=out_hbm.at[pl.ds(token, 1)],
-                send_sem=last_send.at[token],
-                recv_sem=last_recv.at[token],
-                device_id=along_seq(last_offset(OFFSETS[token])),
-                device_id_type=MESH,
-            )
-            copy.start()
-            lasts.append(copy)
+    pl.semaphore_wait(far_sem, 2)
+
+    def token(place, device):
+        return pltpu.make_async_remote_copy(
+            src_ref=outgoing.at[pl.ds(place, 1)],
+            dst_ref=out_hbm.at[pl.ds(place, 1)],
+            send_sem=token_send.at[place],
+            recv_sem=token_recv.at[place],
+            device_id=device,
+            device_id_type=MESH,
+        )
+
+    first_leg = pltpu.make_async_remote_copy(
+        src_ref=outgoing.at[pl.ds(25, 2)],
+        dst_ref=relay,
+        send_sem=relay_send,
+        recv_sem=relay_recv,
+        device_id=along_seq(RELAY),
+        device_id_type=MESH,
+    )
+    first_leg.start()
+    token(24, along_seq(32)).start()
+
+    wrapping = jnp.clip(me - 40, 0, 23)
+    low = jnp.clip(me - 8, 0, 21)
+
+    def up(i):
+        return jnp.where(i < wrapping, SEQ - me + i, jnp.minimum(SEQ - 1 - me, 23) - (i - wrapping))
+
+    def down(i):
+        return jnp.where(i < low, 8 + low - i, 29 - (i - low))
+
+    def send_up(i):
+        offset = up(i)
+        token(offset, along_seq(offset)).start()
+
+    @pl.loop(0, 21)
+    def _(i):
+        send_up(i)
+        offset = down(i)
+        token(18 + offset, along_seq(-offset)).start()
+
+    send_up(21)
+    send_up(22)
+    first_leg.wait_recv()
+    for q in range(2):
+        pltpu.make_async_remote_copy(
+            src_ref=relay.at[pl.ds(q, 1)],
+            dst_ref=out_hbm.at[pl.ds(25 + q, 1)],
+            send_sem=token_send.at[25 + q],
+            recv_sem=token_recv.at[25 + q],
+            device_id=along_seq(RELAY + 1 + q),
+            device_id_type=MESH,
+        ).start()
     own.wait()
-    for copy in jumps.values():
-        copy.wait_send()
-    for copy in lasts:
-        copy.wait()
+    first_leg.wait_send()
+
+    @pl.loop(1, TOK)
+    def _(place):
+        token(place, along_seq(1)).wait()
 
 
 def place_kernel(row_ref, arrived_ref, out_ref):
@@ -342,14 +283,15 @@
             pltpu.VMEM((WIN, D), jnp.bfloat16),
             pltpu.VMEM((4 * WIN, D), jnp.bfloat16),
             pltpu.VMEM((TOK, 8, HALF), jnp.bfloat16),
-            pltpu.VMEM((ROUNDS, TOK, 8, HALF), jnp.bfloat16),
+            pltpu.VMEM((2, 8, HALF), jnp.bfloat16),
             dma((3,)),
             dma((2,)),
-            dma((len(GROUPS) * ROUNDS,)),
-            dma((len(GROUPS) * ROUNDS,)),
+            dma,
+            dma,
             dma((TOK,)),
             dma((TOK,)),
             dma,
+            pltpu.SemaphoreType.REGULAR,
         ],
         compiler_params=pltpu.CompilerParams(collective_id=0, has_side_effects=True),
     )(
@@ -359,8 +301,8 @@
         send_count,
         send_slot,
         out_weight,
-        out_bias.reshape(1, D),
-        norm_gain.reshape(1, D),
+        out_bias,
+        norm_gain,
     )
     placed = pl.pallas_call(
         place_kernel,

time: 88.9 us -> 84.7 us (0.953)
  local copies, waits for them, and re-layouts: 2.57 us -> 0 us
  Pallas kernels: 84.7 us -> 83.2 us
    reshape x2 -> x0, local copies, waits for them, and re-layouts: 2.57 us -> none  [the longest x1 1.28 us: per_device(): out_bias.reshape(1, D)]
    pallas_call x1, Pallas kernels: 82 us -> 80.5 us  [per_device(): pl.pallas_call(encode_kernel, out_shape=jax.ShapeDtypeStruct((TOK, 8, HAL...]
where the time goes in v2:
time: 84.7 us; the launch traced here: 84.5 us
  Pallas kernels  83.2 us (98%)
  between operations  1.3 us (2%)
    pallas_call x1, Pallas kernels, per_device(): pl.pallas_call(encode_kernel, out_shape=jax.ShapeDtypeStruct((TOK, 8, HAL...  80.5 us
    pallas_call x1, Pallas kernels, per_device(): pl.pallas_call(place_kernel, out_shape=jax.ShapeDtypeStruct((TOK, 4 * D),...  2.72 us

profile of v2, /device:TPU:1, one launch (start us, length us, event | category | flops | bytes accessed | tf_op | source)
XLA Modules:
  0.0 84.5 jit_solution(5898040781168116676)
XLA Ops:
  1.3 80.5 %shard_map.91.arrived_ref = bf16[48,8,640]{2,1,0:T(8,128)(2,1)} custom-call(bf16[4,64,3840]{2,1,0:T(8,128)(2,1)} %qkv_hbm.1, bf16[4,64,1280]{2,1,0:T(8,128)(2,1)} %resid_hbm.1, s32[1,1]{1,0:T(1,128)S(6)} %copy.10.count_ref, s32[1,1]{1,0:T(1,128)S(6)} %copy.11.lent_ref, s32[1,48]{1,0:T(1,128)} %slot_ref.1, bf16[1280,1280]{1,0:T(8,128)(2,1)} %weight_hbm.1, ...), custom_call_target="tpu_custom_call" | custom-call | tf_op jit(solution)/shard_map/pallas_call | solution.py:273
  81.8 2.7 %shard_map.92 = bf16[48,5120]{1,0:T(8,128)(2,1)} custom-call(s32[1,64]{1,0:T(1,128)} %row_ref.1, bf16[48,8,640]{2,1,0:T(8,128)(2,1)} %shard_map.91.arrived_ref), custom_call_target="tpu_custom_call" | custom-call | tf_op jit(solution)/shard_map/pallas_call | solution.py:307

commit v3 on v2

--- a/solution.py
+++ b/solution.py
@@ -17,7 +17,10 @@
 ENC = 16
 TOK = 48
 RELAY = 16
-NEAR = [d for d in range(-RELAY, RELAY + 1) if d]
+STEP = 8
+NEAR = [d for d in range(-STEP, STEP + 1) if d]
+
+RELAYED = ((25, 2), (47, 1))
 
 
 def place_offset(place):
@@ -49,6 +52,7 @@
     token_send,
     token_recv,
     own_sem,
+    step_sem,
     far_sem,
 ):
     me = lax.axis_index("seq")
@@ -143,12 +147,13 @@
 
     loads[0].wait()
     attend(last_live, 0)
+    pl.semaphore_wait(barrier, len(NEAR) + 1)
+    for offset in (STEP, -STEP):
+        pl.semaphore_signal(step_sem, inc=1, device_id=along_seq(offset), device_id_type=MESH)
     loads[1].wait()
     loads[2].wait()
     lend[...] = project(WIN, resid[last_live])
 
-    attend(0, 0)
-    pl.semaphore_wait(barrier, len(NEAR) + 1)
     lending = pltpu.make_async_remote_copy(
         src_ref=lend,
         dst_ref=normed.at[pl.ds(3 * WIN, WIN)],
@@ -158,6 +163,9 @@
         device_id_type=MESH,
     )
     lending.start()
+
+    attend(0, 0)
+    pl.semaphore_wait(step_sem, 2)
     for offset in (RELAY, -RELAY):
         pl.semaphore_signal(far_sem, inc=1, device_id=along_seq(offset), device_id_type=MESH)
 
@@ -172,9 +180,17 @@
     pick_low = (hit & ((r & 4) == 0)).astype(jnp.bfloat16)
     pick_high = (hit & ((r & 4) != 0)).astype(jnp.bfloat16)
 
+    def picked(rows):
+        low_half = jnp.dot(
+            pick_low[:, rows], normed[rows, :HALF], preferred_element_type=jnp.float32
+        )
+        return low_half + jnp.dot(
+            pick_high[:, rows], normed[rows, HALF:], preferred_element_type=jnp.float32
+        )
+
+    placed = picked(slice(0, 2 * WIN))
     lending.wait()
-    placed = jnp.dot(pick_low, normed[:, :HALF], preferred_element_type=jnp.float32)
-    placed = placed + jnp.dot(pick_high, normed[:, HALF:], preferred_element_type=jnp.float32)
+    placed = placed + picked(slice(2 * WIN, 4 * WIN))
     outgoing[...] = placed.astype(jnp.bfloat16).reshape(TOK, 8, HALF)
 
     own = pltpu.make_async_copy(outgoing.at[0], out_hbm.at[0], own_sem)
@@ -192,50 +208,56 @@
             device_id_type=MESH,
         )
 
-    first_leg = pltpu.make_async_remote_copy(
-        src_ref=outgoing.at[pl.ds(25, 2)],
-        dst_ref=relay,
-        send_sem=relay_send,
-        recv_sem=relay_recv,
-        device_id=along_seq(RELAY),
-        device_id_type=MESH,
-    )
-    first_leg.start()
+    first_legs = []
+    for leg, (place, count) in enumerate(RELAYED):
+        first_legs.append(
+            pltpu.make_async_remote_copy(
+                src_ref=outgoing.at[pl.ds(place, count)],
+                dst_ref=relay.at[pl.ds(2 * leg, count)],
+                send_sem=relay_send.at[leg],
+                recv_sem=relay_recv.at[leg],
+                device_id=along_seq(RELAY),
+                device_id_type=MESH,
+            )
+        )
+        first_legs[-1].start()
     token(24, along_seq(32)).start()
 
     wrapping = jnp.clip(me - 40, 0, 23)
-    low = jnp.clip(me - 8, 0, 21)
+    low = jnp.clip(me - 8, 0, 20)
 
     def up(i):
         return jnp.where(i < wrapping, SEQ - me + i, jnp.minimum(SEQ - 1 - me, 23) - (i - wrapping))
 
     def down(i):
-        return jnp.where(i < low, 8 + low - i, 29 - (i - low))
-
-    def send_up(i):
+        return jnp.where(i < low, 8 + low - i, 28 - (i - low))
+
+    @pl.loop(0, 20)
+    def _(i):
+        offset = down(i)
+        token(18 + offset, along_seq(-offset)).start()
+
+    for leg, (place, count) in enumerate(RELAYED):
+        first_legs[leg].wait_recv()
+        for q in range(count):
+            held = 2 * leg + q
+            pltpu.make_async_remote_copy(
+                src_ref=relay.at[pl.ds(held, 1)],
+                dst_ref=out_hbm.at[pl.ds(place + q, 1)],
+                send_sem=token_send.at[place + q],
+                recv_sem=token_recv.at[place + q],
+                device_id=along_seq(33 + held - RELAY),
+                device_id_type=MESH,
+            ).start()
+
+    @pl.loop(0, 23)
+    def _(i):
         offset = up(i)
         token(offset, along_seq(offset)).start()
 
-    @pl.loop(0, 21)
-    def _(i):
-        send_up(i)
-        offset = down(i)
-        token(18 + offset, along_seq(-offset)).start()
-
-    send_up(21)
-    send_up(22)
-    first_leg.wait_recv()
-    for q in range(2):
-        pltpu.make_async_remote_copy(
-            src_ref=relay.at[pl.ds(q, 1)],
-            dst_ref=out_hbm.at[pl.ds(25 + q, 1)],
-            send_sem=token_send.at[25 + q],
-            recv_sem=token_recv.at[25 + q],
-            device_id=along_seq(RELAY + 1 + q),
-            device_id_type=MESH,
-        ).start()
     own.wait()
-    first_leg.wait_send()
+    for leg in first_legs:
+        leg.wait_send()
 
     @pl.loop(1, TOK)
     def _(place):
@@ -255,12 +277,13 @@
     c = lax.broadcasted_iota(jnp.int32, (TOK, rows), 1)
     hit = r == row_of
     arrived = arrived_ref[...].reshape(rows, HALF)
+    pick = jnp.concatenate(
+        [(hit & ((c & 7) == part)).astype(jnp.bfloat16) for part in range(8)], axis=0
+    )
+    cut = jnp.dot(pick, arrived, preferred_element_type=jnp.float32).astype(jnp.bfloat16)
     for part in range(8):
-        half, patch = part // 4, part % 4
-        pick = (hit & ((c & 7) == part)).astype(jnp.bfloat16)
-        cut = jnp.dot(pick, arrived, preferred_element_type=jnp.float32)
-        at = patch * D + half * HALF
-        out_ref[:, at : at + HALF] = cut.astype(jnp.bfloat16)
+        at = part % 4 * D + part // 4 * HALF
+        out_ref[:, at : at + HALF] = cut[TOK * part : TOK * (part + 1)]
 
 
 def per_device(
@@ -283,14 +306,15 @@
             pltpu.VMEM((WIN, D), jnp.bfloat16),
             pltpu.VMEM((4 * WIN, D), jnp.bfloat16),
             pltpu.VMEM((TOK, 8, HALF), jnp.bfloat16),
-            pltpu.VMEM((2, 8, HALF), jnp.bfloat16),
+            pltpu.VMEM((3, 8, HALF), jnp.bfloat16),
             dma((3,)),
             dma((2,)),
-            dma,
-            dma,
+            dma((2,)),
+            dma((2,)),
             dma((TOK,)),
             dma((TOK,)),
             dma,
+            pltpu.SemaphoreType.REGULAR,
             pltpu.SemaphoreType.REGULAR,
         ],
         compiler_params=pltpu.CompilerParams(collective_id=0, has_side_effects=True),

time: 84.7 us -> 79.5 us (0.939)
  the two profiles are of different devices: /device:TPU:1 before, /device:TPU:193 now
where the time goes in v3:
time: 79.5 us; the launch traced here: 79.3 us
  Pallas kernels  78 us (98%)
  between operations  1.3 us (2%)
    pallas_call x1, Pallas kernels, per_device(): pl.pallas_call(encode_kernel, out_shape=jax.ShapeDtypeStruct((TOK, 8, HAL...  75.6 us
    pallas_call x1, Pallas kernels, per_device(): pl.pallas_call(place_kernel, out_shape=jax.ShapeDtypeStruct((TOK, 4 * D),...  2.38 us

profile of v3, /device:TPU:193, one launch (start us, length us, event | category | flops | bytes accessed | tf_op | source)
XLA Modules:
  0.0 79.3 jit_solution(3853499412846718434)
XLA Ops:
  1.3 75.6 %shard_map.91.arrived_ref = bf16[48,8,640]{2,1,0:T(8,128)(2,1)} custom-call(bf16[4,64,3840]{2,1,0:T(8,128)(2,1)} %qkv_hbm.1, bf16[4,64,1280]{2,1,0:T(8,128)(2,1)} %resid_hbm.1, s32[1,1]{1,0:T(1,128)S(6)} %copy.10.count_ref, s32[1,1]{1,0:T(1,128)S(6)} %copy.11.lent_ref, s32[1,48]{1,0:T(1,128)} %slot_ref.1, bf16[1280,1280]{1,0:T(8,128)(2,1)} %weight_hbm.1, ...), custom_call_target="tpu_custom_call" | custom-call | tf_op jit(solution)/shard_map/pallas_call | solution.py:296
  76.9 2.4 %shard_map.92 = bf16[48,5120]{1,0:T(8,128)(2,1)} custom-call(s32[1,64]{1,0:T(1,128)} %row_ref.1, bf16[48,8,640]{2,1,0:T(8,128)(2,1)} %shard_map.91.arrived_ref), custom_call_target="tpu_custom_call" | custom-call | tf_op jit(solution)/shard_map/pallas_call | solution.py:331

commit v4 on v3

--- a/solution.py
+++ b/solution.py
@@ -37,6 +37,7 @@
     bias_ref,
     gain_ref,
     out_hbm,
+    first_qkv,
     qkv,
     resid,
     weight,
@@ -69,17 +70,19 @@
         pl.semaphore_signal(barrier, inc=1, device_id=along_seq(offset), device_id_type=MESH)
     pl.semaphore_signal(barrier, inc=1, device_id=prev_enc, device_id_type=MESH)
 
+    later = pl.ds(1, 3)
     loads = [
-        pltpu.make_async_copy(qkv_hbm, qkv, load_sem.at[0]),
+        pltpu.make_async_copy(qkv_hbm.at[later], qkv, load_sem.at[0]),
         pltpu.make_async_copy(weight_hbm, weight, load_sem.at[1]),
         pltpu.make_async_copy(resid_hbm, resid, load_sem.at[2]),
+        pltpu.make_async_copy(qkv_hbm.at[pl.ds(0, 1)], first_qkv, load_sem.at[3]),
     ]
     for copy in loads:
         copy.start()
 
     live = count_ref[0, 0]
     kept = live - lent_ref[0, 0]
-    last_live = jnp.clip(live - 1, 0, 3)
+    last_live = jnp.clip(live - 1, 1, 3)
     bias = bias_ref[...].astype(jnp.float32).reshape(1, D)
     gain = gain_ref[...].astype(jnp.float32).reshape(1, D)
 
@@ -110,7 +113,7 @@
         ones_mask.append(((lane128 >= start) & (lane128 < start + HEAD)).astype(jnp.bfloat16))
     left = lax.broadcasted_iota(jnp.int32, (WIN, 128), 1) < WIN
 
-    def attend(slot, row):
+    def attend(qkv, slot, row):
         for group in range(2):
             num = [None] * 5
             den = [None] * 5
@@ -146,7 +149,7 @@
         return (hidden * inv_rms * gain).astype(jnp.bfloat16)
 
     loads[0].wait()
-    attend(last_live, 0)
+    attend(qkv, last_live - 1, 0)
     pl.semaphore_wait(barrier, len(NEAR) + 1)
     for offset in (STEP, -STEP):
         pl.semaphore_signal(step_sem, inc=1, device_id=along_seq(offset), device_id_type=MESH)
@@ -164,13 +167,14 @@
     )
     lending.start()
 
-    attend(0, 0)
+    loads[3].wait()
+    attend(first_qkv, 0, 0)
     pl.semaphore_wait(step_sem, 2)
     for offset in (RELAY, -RELAY):
         pl.semaphore_signal(far_sem, inc=1, device_id=along_seq(offset), device_id_type=MESH)
 
-    attend(1, WIN)
-    attend(2, 2 * WIN)
+    attend(qkv, 0, WIN)
+    attend(qkv, 1, 2 * WIN)
     normed[0 : 3 * WIN] = project(3 * WIN, resid[0:3].reshape(3 * WIN, D))
 
     r = lax.broadcasted_iota(jnp.int32, (TOK * 8, 4 * WIN), 0)
@@ -295,11 +299,12 @@
     dma = pltpu.SemaphoreType.DMA
     arrived = pl.pallas_call(
         encode_kernel,
-        out_shape=jax.ShapeDtypeStruct((TOK, 8, HALF), jnp.bfloat16),
+        out_shape=pltpu.VMEM((TOK, 8, HALF), jnp.bfloat16),
         in_specs=[hbm, hbm, smem, smem, vmem, hbm, vmem, vmem],
-        out_specs=hbm,
+        out_specs=vmem,
         scratch_shapes=[
-            pltpu.VMEM(qkv.shape, jnp.bfloat16),
+            pltpu.VMEM((1,) + qkv.shape[1:], jnp.bfloat16),
+            pltpu.VMEM((3,) + qkv.shape[1:], jnp.bfloat16),
             pltpu.VMEM(resid.shape, jnp.bfloat16),
             pltpu.VMEM((D, D), jnp.bfloat16),
             pltpu.VMEM((3 * WIN, D), jnp.bfloat16),
@@ -307,7 +312,7 @@
             pltpu.VMEM((4 * WIN, D), jnp.bfloat16),
             pltpu.VMEM((TOK, 8, HALF), jnp.bfloat16),
             pltpu.VMEM((3, 8, HALF), jnp.bfloat16),
-            dma((3,)),
+            dma((4,)),
             dma((2,)),
             dma((2,)),
             dma((2,)),
@@ -333,7 +338,7 @@
         out_shape=jax.ShapeDtypeStruct((TOK, 4 * D), jnp.bfloat16),
         in_specs=[vmem, vmem],
         out_specs=vmem,
-    )(lm_row, arrived)
+    )(lm_row, pltpu.with_memory_space_constraint(arrived, pltpu.VMEM))
     return placed[None]
 
 

time: 79.5 us -> 78.9 us (level)
  no operation moved by 1% of the time
where the time goes in v4:
time: 78.9 us; the launch traced here: 78.7 us
  Pallas kernels  77.4 us (98%)
  between operations  1.3 us (2%)
    pallas_call x1, Pallas kernels, per_device(): pl.pallas_call(encode_kernel, out_shape=pltpu.VMEM((TOK, 8, HALF), jnp.bf...  75.4 us
    pallas_call x1, Pallas kernels, per_device(): pl.pallas_call(place_kernel, out_shape=jax.ShapeDtypeStruct((TOK, 4 * D),...  1.99 us

profile of v4, /device:TPU:193, one launch (start us, length us, event | category | flops | bytes accessed | tf_op | source)
XLA Modules:
  0.0 78.7 jit_solution(9648849389624901048)
XLA Ops:
  1.3 75.4 %shard_map.91.arrived_ref = bf16[48,8,640]{2,1,0:T(8,128)(2,1)S(1)} custom-call(bf16[4,64,3840]{2,1,0:T(8,128)(2,1)} %qkv_hbm.1, bf16[4,64,1280]{2,1,0:T(8,128)(2,1)} %resid_hbm.1, s32[1,1]{1,0:T(1,128)S(6)} %copy.10.count_ref, s32[1,1]{1,0:T(1,128)S(6)} %copy.11.lent_ref, s32[1,48]{1,0:T(1,128)} %slot_ref.1, bf16[1280,1280]{1,0:T(8,128)(2,1)} %weight_hbm.1, ...), custom_call_target="tpu_custom_call" | custom-call | tf_op jit(solution)/shard_map/pallas_call | solution.py:300
  76.7 2.0 %shard_map.92 = bf16[48,5120]{1,0:T(8,128)(2,1)} custom-call(s32[1,64]{1,0:T(1,128)} %row_ref.1, bf16[48,8,640]{2,1,0:T(8,128)(2,1)S(1)} %shard_map.91.arrived_ref), custom_call_target="tpu_custom_call" | custom-call | tf_op jit(solution)/shard_map/pallas_call | solution.py:336

commit v5 on v4

--- a/solution.py
+++ b/solution.py
@@ -33,10 +33,12 @@
     count_ref,
     lent_ref,
     slot_ref,
+    row_ref,
     weight_hbm,
     bias_ref,
     gain_ref,
     out_hbm,
+    pick_ref,
     first_qkv,
     qkv,
     resid,
@@ -71,9 +73,11 @@
     pl.semaphore_signal(barrier, inc=1, device_id=prev_enc, device_id_type=MESH)
 
     later = pl.ds(1, 3)
+    top, bottom = pl.ds(0, HALF), pl.ds(HALF, HALF)
     loads = [
         pltpu.make_async_copy(qkv_hbm.at[later], qkv, load_sem.at[0]),
-        pltpu.make_async_copy(weight_hbm, weight, load_sem.at[1]),
+        pltpu.make_async_copy(weight_hbm.at[top], weight.at[top], load_sem.at[1]),
+        pltpu.make_async_copy(weight_hbm.at[bottom], weight.at[bottom], load_sem.at[4]),
         pltpu.make_async_copy(resid_hbm, resid, load_sem.at[2]),
         pltpu.make_async_copy(qkv_hbm.at[pl.ds(0, 1)], first_qkv, load_sem.at[3]),
     ]
@@ -142,8 +146,7 @@
                 at = HALF * group + 128 * tile
                 att[pl.ds(row, WIN), at : at + 128] = (num[tile] / den[tile]).astype(jnp.bfloat16)
 
-    def project(rows, resid_rows):
-        hidden = jnp.dot(att[0:rows], weight[...], preferred_element_type=jnp.float32)
+    def project(hidden, resid_rows):
         hidden = hidden + bias + resid_rows.astype(jnp.float32)
         inv_rms = lax.rsqrt(jnp.mean(hidden * hidden, axis=-1, keepdims=True) + 1e-06)
         return (hidden * inv_rms * gain).astype(jnp.bfloat16)
@@ -154,8 +157,13 @@
     for offset in (STEP, -STEP):
         pl.semaphore_signal(step_sem, inc=1, device_id=along_seq(offset), device_id_type=MESH)
     loads[1].wait()
+    hidden = jnp.dot(att[0:WIN, :HALF], weight[:HALF], preferred_element_type=jnp.float32)
     loads[2].wait()
-    lend[...] = project(WIN, resid[last_live])
+    loads[3].wait()
+    hidden = hidden + jnp.dot(
+        att[0:WIN, HALF:], weight[HALF:], preferred_element_type=jnp.float32
+    )
+    lend[...] = project(hidden, resid[last_live])
 
     lending = pltpu.make_async_remote_copy(
         src_ref=lend,
@@ -167,7 +175,7 @@
     )
     lending.start()
 
-    loads[3].wait()
+    loads[4].wait()
     attend(first_qkv, 0, 0)
     pl.semaphore_wait(step_sem, 2)
     for offset in (RELAY, -RELAY):
@@ -175,7 +183,8 @@
 
     attend(qkv, 0, WIN)
     attend(qkv, 1, 2 * WIN)
-    normed[0 : 3 * WIN] = project(3 * WIN, resid[0:3].reshape(3 * WIN, D))
+    hidden = jnp.dot(att[...], weight[...], preferred_element_type=jnp.float32)
+    normed[0 : 3 * WIN] = project(hidden, resid[0:3].reshape(3 * WIN, D))
 
     r = lax.broadcasted_iota(jnp.int32, (TOK * 8, 4 * WIN), 0)
     c = lax.broadcasted_iota(jnp.int32, (TOK * 8, 4 * WIN), 1)
@@ -184,21 +193,21 @@
     pick_low = (hit & ((r & 4) == 0)).astype(jnp.bfloat16)
     pick_high = (hit & ((r & 4) != 0)).astype(jnp.bfloat16)
 
-    def picked(rows):
+    def picked(places, rows):
         low_half = jnp.dot(
-            pick_low[:, rows], normed[rows, :HALF], preferred_element_type=jnp.float32
+            pick_low[places, rows], normed[rows, :HALF], preferred_element_type=jnp.float32
         )
         return low_half + jnp.dot(
-            pick_high[:, rows], normed[rows, HALF:], preferred_element_type=jnp.float32
+            pick_high[places, rows], normed[rows, HALF:], preferred_element_type=jnp.float32
         )
 
-    placed = picked(slice(0, 2 * WIN))
+    near, far = slice(0, 4 * TOK), slice(4 * TOK, 8 * TOK)
+    own, rest = slice(0, 2 * WIN), slice(2 * WIN, 4 * WIN)
+    placed = picked(far, own)
+    placed_near = picked(near, own)
     lending.wait()
-    placed = placed + picked(slice(2 * WIN, 4 * WIN))
-    outgoing[...] = placed.astype(jnp.bfloat16).reshape(TOK, 8, HALF)
-
-    own = pltpu.make_async_copy(outgoing.at[0], out_hbm.at[0], own_sem)
-    own.start()
+    placed = placed + picked(far, rest)
+    outgoing[TOK // 2 :] = placed.astype(jnp.bfloat16).reshape(TOK // 2, 8, HALF)
 
     pl.semaphore_wait(far_sem, 2)
 
@@ -241,6 +250,9 @@
         offset = down(i)
         token(18 + offset, along_seq(-offset)).start()
 
+    placed_near = placed_near + picked(near, rest)
+    outgoing[0 : TOK // 2] = placed_near.astype(jnp.bfloat16).reshape(TOK // 2, 8, HALF)
+
     for leg, (place, count) in enumerate(RELAYED):
         first_legs[leg].wait_recv()
         for q in range(count):
@@ -259,17 +271,9 @@
         offset = up(i)
         token(offset, along_seq(offset)).start()
 
-    own.wait()
-    for leg in first_legs:
-        leg.wait_send()
-
-    @pl.loop(1, TOK)
-    def _(place):
-        token(place, along_seq(1)).wait()
-
-
-def place_kernel(row_ref, arrived_ref, out_ref):
-    me = lax.axis_index("seq")
+    own_copy = pltpu.make_async_copy(outgoing.at[0], out_hbm.at[0], own_sem)
+    own_copy.start()
+
     rows = TOK * 8
     g = lax.broadcasted_iota(jnp.int32, (SEQ, rows), 0)
     c = lax.broadcasted_iota(jnp.int32, (SEQ, rows), 1)
@@ -280,14 +284,36 @@
     r = lax.broadcasted_iota(jnp.int32, (TOK, rows), 0)
     c = lax.broadcasted_iota(jnp.int32, (TOK, rows), 1)
     hit = r == row_of
-    arrived = arrived_ref[...].reshape(rows, HALF)
-    pick = jnp.concatenate(
-        [(hit & ((c & 7) == part)).astype(jnp.bfloat16) for part in range(8)], axis=0
-    )
-    cut = jnp.dot(pick, arrived, preferred_element_type=jnp.float32).astype(jnp.bfloat16)
     for part in range(8):
-        at = part % 4 * D + part // 4 * HALF
-        out_ref[:, at : at + HALF] = cut[TOK * part : TOK * (part + 1)]
+        pick_ref[TOK * part : TOK * (part + 1)] = (hit & ((c & 7) == part)).astype(jnp.bfloat16)
+
+    own_copy.wait()
+    for leg in first_legs:
+        leg.wait_send()
+
+    @pl.loop(1, TOK)
+    def _(place):
+        token(place, along_seq(1)).wait()
+
+
+def place_kernel(pick_ref, arrived_ref, out_hbm, staged, sems):
+    arrived = arrived_ref[...].reshape(TOK * 8, HALF)
+    copies = []
+    for half in range(2):
+        rows = slice(4 * TOK * half, 4 * TOK * (half + 1))
+        cut = jnp.dot(pick_ref[rows], arrived, preferred_element_type=jnp.float32)
+        for patch in range(4):
+            part = 4 * half + patch
+            staged[part] = cut[TOK * patch : TOK * (patch + 1)].astype(jnp.bfloat16)
+            at = patch * D + half * HALF
+            copies.append(
+                pltpu.make_async_copy(
+                    staged.at[part], out_hbm.at[:, pl.ds(at, HALF)], sems.at[part]
+                )
+            )
+            copies[-1].start()
+    for copy in copies:
+        copy.wait()
 
 
 def per_device(
@@ -297,11 +323,14 @@
     smem = pl.BlockSpec(memory_space=pltpu.SMEM)
     hbm = pl.BlockSpec(memory_space=pl.ANY)
     dma = pltpu.SemaphoreType.DMA
-    arrived = pl.pallas_call(
+    arrived, pick = pl.pallas_call(
         encode_kernel,
-        out_shape=pltpu.VMEM((TOK, 8, HALF), jnp.bfloat16),
-        in_specs=[hbm, hbm, smem, smem, vmem, hbm, vmem, vmem],
-        out_specs=vmem,
+        out_shape=(
+            pltpu.VMEM((TOK, 8, HALF), jnp.bfloat16),
+            pltpu.VMEM((TOK * 8, TOK * 8), jnp.bfloat16),
+        ),
+        in_specs=[hbm, hbm, smem, smem, vmem, vmem, hbm, vmem, vmem],
+        out_specs=(vmem, vmem),
         scratch_shapes=[
             pltpu.VMEM((1,) + qkv.shape[1:], jnp.bfloat16),
             pltpu.VMEM((3,) + qkv.shape[1:], jnp.bfloat16),
@@ -312,7 +341,7 @@
             pltpu.VMEM((4 * WIN, D), jnp.bfloat16),
             pltpu.VMEM((TOK, 8, HALF), jnp.bfloat16),
             pltpu.VMEM((3, 8, HALF), jnp.bfloat16),
-            dma((4,)),
+            dma((5,)),
             dma((2,)),
             dma((2,)),
             dma((2,)),
@@ -329,6 +358,7 @@
         block_count,
         send_count,
         send_slot,
+        lm_row,
         out_weight,
         out_bias,
         norm_gain,
@@ -337,8 +367,12 @@
         place_kernel,
         out_shape=jax.ShapeDtypeStruct((TOK, 4 * D), jnp.bfloat16),
         in_specs=[vmem, vmem],
-        out_specs=vmem,
-    )(lm_row, pltpu.with_memory_space_constraint(arrived, pltpu.VMEM))
+        out_specs=hbm,
+        scratch_shapes=[pltpu.VMEM((8, TOK, HALF), jnp.bfloat16), dma((8,))],
+    )(
+        pltpu.with_memory_space_constraint(pick, pltpu.VMEM),
+        pltpu.with_memory_space_constraint(arrived, pltpu.VMEM),
+    )
     return placed[None]
 
 

time: 78.9 us -> 78.4 us (level)
    pallas_call x1, Pallas kernels: 1.99 us -> 1.18 us  [per_device(): pl.pallas_call(place_kernel, out_shape=jax.ShapeDtypeStruct((TOK, 4 * D),...]
where the time goes in v5:
time: 78.4 us; the launch traced here: 78.2 us
  Pallas kernels  76.9 us (98%)
  between operations  1.3 us (2%)
    pallas_call x1, Pallas kernels, per_device(): pl.pallas_call(encode_kernel, out_shape=(pltpu.VMEM((TOK, 8, HALF), jnp.b...  75.7 us

profile of v5, /device:TPU:193, one launch (start us, length us, event | category | flops | bytes accessed | tf_op | source)
XLA Modules:
  0.0 78.2 jit_solution(13747073374580192176)
XLA Ops:
  1.3 75.7 %shard_map.91 = (bf16[48,8,640]{2,1,0:T(8,128)(2,1)S(1)}, bf16[384,384]{1,0:T(8,128)(2,1)S(1)}) custom-call(bf16[4,64,3840]{2,1,0:T(8,128)(2,1)} %qkv_hbm.1, bf16[4,64,1280]{2,1,0:T(8,128)(2,1)} %resid_hbm.1, s32[1,1]{1,0:T(1,128)S(6)} %copy.10.count_ref, s32[1,1]{1,0:T(1,128)S(6)} %copy.11.lent_ref, s32[1,48]{1,0:T(1,128)} %slot_ref.1, s32[1,64]{1,0:T(1,128)} %row_ref.1, ...), custom_call_target="tpu_custom_call" | custom-call | tf_op jit(solution)/shard_map/pallas_call | solution.py:326
  77.0 1.2 %shard_map.92 = bf16[48,5120]{1,0:T(8,128)(2,1)} custom-call(bf16[384,384]{1,0:T(8,128)(2,1)S(1)} %get-tuple-element.7.pick_ref, bf16[48,8,640]{2,1,0:T(8,128)(2,1)S(1)} %get-tuple-element.8.arrived_ref), custom_call_target="tpu_custom_call" | custom-call | tf_op jit(solution)/shard_map/pallas_call | solution.py:366

commit v6 on v5

--- a/solution.py
+++ b/solution.py
@@ -245,7 +245,7 @@
     def down(i):
         return jnp.where(i < low, 8 + low - i, 28 - (i - low))
 
-    @pl.loop(0, 20)
+    @pl.loop(0, 20, unroll=True)
     def _(i):
         offset = down(i)
         token(18 + offset, along_seq(-offset)).start()
@@ -266,7 +266,7 @@
                 device_id_type=MESH,
             ).start()
 
-    @pl.loop(0, 23)
+    @pl.loop(0, 23, unroll=True)
     def _(i):
         offset = up(i)
         token(offset, along_seq(offset)).start()

time: 78.4 us -> 78.4 us (level)
  no operation moved by 1% of the time
where the time goes in v6:
time: 78.4 us; the launch traced here: 78.2 us
  Pallas kernels  76.9 us (98%)
  between operations  1.3 us (2%)
    pallas_call x1, Pallas kernels, per_device(): pl.pallas_call(encode_kernel, out_shape=(pltpu.VMEM((TOK, 8, HALF), jnp.b...  75.7 us

profile of v6, /device:TPU:193, one launch (start us, length us, event | category | flops | bytes accessed | tf_op | source)
XLA Modules:
  0.0 78.2 jit_solution(4634643078148528122)
XLA Ops:
  1.3 75.7 %shard_map.91 = (bf16[48,8,640]{2,1,0:T(8,128)(2,1)S(1)}, bf16[384,384]{1,0:T(8,128)(2,1)S(1)}) custom-call(bf16[4,64,3840]{2,1,0:T(8,128)(2,1)} %qkv_hbm.1, bf16[4,64,1280]{2,1,0:T(8,128)(2,1)} %resid_hbm.1, s32[1,1]{1,0:T(1,128)S(6)} %copy.10.count_ref, s32[1,1]{1,0:T(1,128)S(6)} %copy.11.lent_ref, s32[1,48]{1,0:T(1,128)} %slot_ref.1, s32[1,64]{1,0:T(1,128)} %row_ref.1, ...), custom_call_target="tpu_custom_call" | custom-call | tf_op jit(solution)/shard_map/pallas_call | solution.py:326
  77.0 1.2 %shard_map.92 = bf16[48,5120]{1,0:T(8,128)(2,1)} custom-call(bf16[384,384]{1,0:T(8,128)(2,1)S(1)} %get-tuple-element.7.pick_ref, bf16[48,8,640]{2,1,0:T(8,128)(2,1)S(1)} %get-tuple-element.8.arrived_ref), custom_call_target="tpu_custom_call" | custom-call | tf_op jit(solution)/shard_map/pallas_call | solution.py:366
